TPU v7x, 512 devices: a whole 4x4x16 slice. The times are simulated.
512 devices in a mesh: blk: 32 (over y, x, core), int: 16 (over z).
Axes of the slice: x: 4, y: 4, z: 16, core: 2. Of those that a mesh axis runs over, the one named last changes fastest.
Arguments:
- amplitudes: float32 [4, 608, 64, 608], P(None, 'blk', 'int'), may hold values from -6 to 6
- integrals: float32 [64, 608, 4, 608], P('int', None, None, 'blk'), may hold values from -0.078125 to 0.078125
- occ_irrep: int32 [64], replicated, may hold values from 0 to 7
- virt_irrep: int32 [608], replicated, may hold values from 0 to 7, as said below
- i_batch: int32 [4], replicated, may hold values from 0 to 63
- j_batch: int32 [4], replicated, may hold values from 0 to 63
Outputs:
- residual: float32 [4, 608, 4, 608], P(None, 'blk', None, 'int')
Inputs may be any that keep to these rules, and one draw needn't show every extreme that they name: `occ_irrep`: labels of the eight D2h irreps; the product of two irreps is the bitwise exclusive or of their labels. `virt_irrep`: labels of the eight D2h irreps, combined as above; no irrep labels more than 96 virtual orbitals, and one labels exactly 96. `i_batch`: positions among the 64 occupied orbitals. `j_batch`: positions among the 64 occupied orbitals.
All inputs are finite; a program needn't handle non-finite values.
Results may differ from a plain program's by a relative error of at most 0.00007.
Values sent between devices are 32-bit elements; how exact they have to be, the bound alone decides.
A program may use at most 128 MiB of HBM per device.

v0:
```python
import jax
import jax.numpy as jnp
from jax import lax
from jax.sharding import PartitionSpec as P


def lookup(labels, where_at):
    positions = jnp.arange(labels.shape[0], dtype=jnp.int32)
    onehot = (where_at[:, None] == positions[None, :]).astype(jnp.int32)
    return jnp.sum(onehot * labels[None, :], axis=1)


def per_device(amplitudes, integrals, occ_irrep, virt_irrep, i_batch, j_batch):
    a_count = amplitudes.shape[1]
    k_count = amplitudes.shape[2]
    a_start = lax.axis_index("blk") * a_count
    k_start = lax.axis_index("int") * k_count
    occ_k = lax.dynamic_slice_in_dim(occ_irrep, k_start, k_count)
    virt_a = lax.dynamic_slice_in_dim(virt_irrep, a_start, a_count)
    irr_i = lookup(occ_irrep, i_batch)
    irr_j = lookup(occ_irrep, j_batch)
    left_pair = jnp.bitwise_xor(irr_i[:, None, None, None], occ_k[None, None, :, None])
    amp_keep = left_pair == jnp.bitwise_xor(
        virt_a[None, :, None, None], virt_irrep[None, None, None, :]
    )
    swap_keep = left_pair == jnp.bitwise_xor(
        virt_irrep[None, :, None, None], virt_a[None, None, None, :]
    )
    sym_amp = jnp.where(amp_keep, amplitudes, 0.0)
    moved = lax.all_to_all(amplitudes, "blk", split_axis=3, concat_axis=1, tiled=True)
    sym_moved = jnp.where(swap_keep, moved, 0.0)
    occ_virt = jnp.bitwise_xor(occ_k[:, None, None, None], virt_irrep[None, :, None, None])
    int_keep = occ_virt == jnp.bitwise_xor(
        irr_j[None, None, :, None], virt_irrep[None, None, None, :]
    )
    sym_piece = jnp.where(int_keep, lax.all_gather(integrals, "blk", axis=3, tiled=True), 0.0)
    cycle = jnp.einsum("iakc,kcjb->iajb", sym_amp, sym_piece, precision=lax.Precision.HIGHEST)
    swapped = jnp.einsum("icka,kcjb->iajb", sym_moved, sym_piece, precision=lax.Precision.HIGHEST)
    terms = jnp.stack((cycle, swapped))
    summed = lax.psum_scatter(terms, "int", scatter_dimension=4, tiled=True)
    return 2.0 * summed[0] - summed[1]


def solution(mesh):
    placed = (P(None, "blk", "int", None), P("int", None, None, "blk"), P(), P(), P(), P())
    return jax.shard_map(
        per_device,
        mesh=mesh,
        in_specs=placed,
        out_specs=P(None, "blk", None, "int"),
        check_vma=False,
    )
```

profile of v0, /device:TPU:2, one launch (start us, length us, event | category | flops | bytes accessed | tf_op | source)
XLA Modules:
  0.0 368.6 jit_solution(17444483353083959431)
XLA Ops:
  6.5 0.0 all-gather.2.cloned.1.call-start
  6.5 0.7 all-gather.2.cloned.1.call-update
  7.3 4.9 %copy.50 = f32[4,19,4,608]{1,2,0,3:T(4,128)} copy(f32[4,19,4,608]{3,2,1,0:T(4,128)} %param.6) | data formatting | bytes 1478656 | tf_op args[0]
  12.1 7.6 %reshape.168 = f32[32,1,5776]{2,1,0:T(1,128)} reshape(f32[608,4,4,19]{3,2,1,0:T(4,128)} %bitcast.42) | data formatting | bytes 1478656
  19.8 9.5 %all-to-all-start = ((f32[32,1,5776]{2,1,0:T(1,128)}), f32[32,1,5776]{2,1,0:T(1,128)S(1)}, u32[]{:S(2)}, u32[]{:S(2)}) async-start(f32[32,1,5776]{2,1,0:T(1,128)} %reshape.168), calls=%async_computation | async-start | bytes 1507328 | tf_op jit(solution)/shard_map/all_to_all | solution.py:30
  29.2 0.0 all-reduce.3.cloned.1.call-start
  29.3 0.7 dynamic_slice.6
  30.0 0.9 select_reduce_fusion.1
  30.9 0.8 broadcast_xor_fusion.3
  31.7 0.2 copy.47
  31.9 0.8 dynamic_slice.7
  32.6 0.1 broadcast_xor_fusion.4
  32.7 0.8 broadcast_xor_fusion
  33.5 0.8 broadcast_xor_fusion.1
  34.2 1.4 select_bitcast_fusion.1
  35.7 10.2 %all-to-all-done = f32[32,1,5776]{2,1,0:T(1,128)S(1)} async-done(((f32[32,1,5776]{2,1,0:T(1,128)}), f32[32,1,5776]{2,1,0:T(1,128)S(1)}, u32[]{:S(2)}, u32[]{:S(2)}) %all-to-all-start) | async-done | bytes 739360 | tf_op jit(solution)/shard_map/all_to_all | solution.py:30
  45.9 0.5 broadcast.124
  46.4 2.4 reduce
  48.9 8.0 %reshape.169 = f32[608,4,4,19]{3,2,1,0:T(4,128)} reshape(f32[32,5776]{1,0:T(8,128)S(1)} %reduce) | data formatting | bytes 1478656
  56.9 6.2 %copy.73 = f32[4,19,4,32,19]{1,3,2,4,0:T(8,128)} copy(f32[4,19,4,32,19]{1,2,0,4,3:T(4,128)} %bitcast.40) | data formatting | bytes 1478656 | tf_op jit(solution)/shard_map/all_to_all | solution.py:30
  63.1 6.0 %all_to_all.16 = f32[4,608,4,19]{1,2,3,0:T(4,128)S(1)} reshape(f32[4,32,19,4,19]{2,1,3,4,0:T(8,128)} %bitcast.41) | data formatting | bytes 1478656 | tf_op jit(solution)/shard_map/all_to_all | solution.py:30
  69.1 0.3 select_bitcast_fusion
  69.4 57.0 %all-gather.2.cloned.1.call-done = f32[4,608,4,608]{1,2,3,0:T(4,128)} async-done(((f32[4,608,4,19]{1,2,3,0:T(4,128)}), f32[4,608,4,608]{1,2,3,0:T(4,128)}) %all-gather.2.cloned.1.call-update) | async-done | bytes 23658512 | tf_op jit(solution)/shard_map/all_gather | solution.py:36
  126.3 22.7 %compare_select_fusion = f32[4,608,4,608]{1,2,3,0:T(4,128)} fusion(f32[4,608,4,608]{1,2,3,0:T(4,128)} %all-gather.2.cloned.1.call-done, s32[4,608]{0,1:T(8,128)S(1)} %copy.47, s32[4,608]{1,0:T(4,128)S(1)} %get-tuple-element.7), kind=kLoop, calls=%fused_computation.4 | loop fusion | flops 11829248 | bytes 47336448 | tf_op jit(solution)/shard_map/jit(_where)/select_n | solution.py:36
  149.0 30.2 %copy.49 = f32[4,608,4,608]{3,1,0,2:T(8,128)} copy(f32[4,608,4,608]{1,2,3,0:T(4,128)} %compare_select_fusion) | data formatting | bytes 47316992 | tf_op jit(solution)/shard_map/jit(_where)/select_n | solution.py:36
  179.2 18.0 %fusion.7 = f32[1,4,19,4,608]{4,2,3,1,0:T(8,128)S(1)} fusion(f32[4,608,4,608]{3,1,0,2:T(8,128)} %copy.49, f32[4,608,4,19,1]{1,2,3,0,4:T(4,128)S(1)} %select_bitcast_fusion), kind=kOutput, calls=%fused_computation.8 | convolution fusion | flops 5394137088 | bytes 25137152 | tf_op jit(solution)/shard_map/icka,kcjb->iajb/dot_general | solution.py:38
  197.3 18.1 %fusion.4 = f32[1,4,19,4,608]{4,2,3,1,0:T(8,128)S(1)} fusion(f32[4,608,4,608]{3,1,0,2:T(8,128)} %copy.49, f32[4,19,4,608,1]{3,2,1,0,4:T(4,128)S(1)} %select_bitcast_fusion.1), kind=kOutput, calls=%fused_computation.7 | convolution fusion | flops 5394137088 | bytes 25137152 | tf_op jit(solution)/shard_map/iakc,kcjb->iajb/dot_general | solution.py:37
  215.4 1.4 pad_maximum_fusion
  216.8 0.0 all-reduce.3.cloned.1.call-update
  216.8 1.3 dynamic-slice
  218.7 141.1 %all-reduce.3.cloned.1.call-done = f32[2,4,19,4,608]{4,2,3,1,0:T(8,128)} async-done(((f32[2,4,19,4,608]{4,2,3,1,0:T(8,128)}), f32[2,4,19,4,608]{4,2,3,1,0:T(8,128)}) %all-reduce.3.cloned.1.call-update) | async-done | bytes 1478672
  359.8 1.3 fusion.12
  361.1 0.7 copy.55
Async XLA Ops:
  6.5 119.8 %all-gather.2.cloned.1.call-start = ((), (), s32[]{:S(2)}) async-start(), calls=%async_computation.1 | async-start | bytes 25681920 | tf_op jit(solution)/shard_map/all_gather | solution.py:36
  19.8 26.2 %all-to-all-start = ((f32[32,1,5776]{2,1,0:T(1,128)}), f32[32,1,5776]{2,1,0:T(1,128)S(1)}, u32[]{:S(2)}, u32[]{:S(2)}) async-start(f32[32,1,5776]{2,1,0:T(1,128)} %reshape.168), calls=%async_computation | async-start | bytes 1507328 | tf_op jit(solution)/shard_map/all_to_all | solution.py:30
  29.2 330.6 %all-reduce.3.cloned.1.call-start = ((), (), s32[]{:S(2)}) async-start(), calls=%async_computation.2 | async-start | bytes 3932160
Sparse Core Ops, SparseCore 0:
  10.6 115.7 all-gather.1
  216.9 142.8 all-reduce.2
where the time goes:
time: 370 us; the launch traced here: 369 us
  waiting for transfers between devices  209 us (56%)
  local copies, waits for them, and re-layouts  67.1 us (18%)
  matrix products  36.1 us (10%)
  other arithmetic  32.8 us (9%)
  between operations  14.1 us (4%)
  starting transfers between devices  9.52 us (3%)
    unnamed x3, waiting for transfers between devices  142 us
    all_gather x1, waiting for transfers between devices, per_device(): lax.all_gather(integrals, 'blk', axis=3, tiled=True)  57 us
    select_n x1, local copies, waits for them, and re-layouts, per_device(): jnp.where(int_keep, lax.all_gather(integrals, 'blk', axis=3, tiled=True),...  30.2 us
    select_n x1, other arithmetic, per_device(): jnp.where(int_keep, lax.all_gather(integrals, 'blk', axis=3, tiled=True),...  22.7 us
    unnamed x4, local copies, waits for them, and re-layouts  21.8 us
    dot_general x1, matrix products, per_device(): jnp.einsum('iakc,kcjb->iajb', sym_amp, sym_piece, precision=lax.Precision...  18.1 us
    dot_general x1, matrix products, per_device(): jnp.einsum('icka,kcjb->iajb', sym_moved, sym_piece, precision=lax.Precisi...  18 us
    all_to_all x3, local copies, waits for them, and re-layouts, per_device(): lax.all_to_all(amplitudes, 'blk', split_axis=3, concat_axis=1, tiled=True)  12.7 us
  transfers between devices with their start and end apart: 3, of which 3 were waited for; matrix products, arithmetic and copies ran while one was open for 10% of the time, Pallas kernels for 0%

commit v1 on v0

--- a/solution.py
+++ b/solution.py
@@ -33,7 +33,13 @@
     int_keep = occ_virt == jnp.bitwise_xor(
         irr_j[None, None, :, None], virt_irrep[None, None, None, :]
     )
-    sym_piece = jnp.where(int_keep, lax.all_gather(integrals, "blk", axis=3, tiled=True), 0.0)
+    sym_piece = jnp.where(
+        int_keep,
+        jnp.concatenate(
+            lax.all_to_all(jnp.stack([integrals] * lax.axis_size("blk")), "blk", 0, 0), axis=3
+        ),
+        0.0,
+    )
     cycle = jnp.einsum("iakc,kcjb->iajb", sym_amp, sym_piece, precision=lax.Precision.HIGHEST)
     swapped = jnp.einsum("icka,kcjb->iajb", sym_moved, sym_piece, precision=lax.Precision.HIGHEST)
     terms = jnp.stack((cycle, swapped))

time: 370 us -> 619 us (1.67)
  waiting for transfers between devices: 209 us -> 433 us
  blocking collectives: 0 us -> 21.6 us
  local copies, waits for them, and re-layouts: 67.1 us -> 88.1 us
  other arithmetic: 32.8 us -> 18.5 us
    all_to_all x1, waiting for transfers between devices: 10.2 us -> 285 us  [per_device(): lax.all_to_all(jnp.stack([integrals] * lax.axis_size('blk')), 'blk', 0, 0)]
    all_gather x1 -> x0, waiting for transfers between devices: 57 us -> none  [per_device(): lax.all_gather(integrals, 'blk', axis=3, tiled=True)]
    all_to_all x0 -> x1, blocking collectives: none -> 21.6 us  [per_device(): lax.all_to_all(amplitudes, 'blk', split_axis=3, concat_axis=1, tiled=True)]
    reshape x0 -> x1, local copies, waits for them, and re-layouts: none -> 13.2 us  [per_device(): jnp.concatenate(lax.all_to_all(jnp.stack([integrals] * lax.axis_size('blk...]
    select_n x1, other arithmetic: 22.7 us -> 12.4 us  [per_device(): jnp.where(int_keep, jnp.concatenate(lax.all_to_all(jnp.stack([integrals]...]
    another operation x0 -> x1, local copies, waits for them, and re-layouts: none -> 9.87 us  [per_device(): jnp.stack([integrals] * lax.axis_size('blk'))]
    unnamed x3 -> x2, waiting for transfers between devices: 142 us -> 148 us
    unnamed x4 -> x14, local copies, waits for them, and re-layouts: 21.8 us -> 21.2 us
  transfers between devices with their start and end apart: 3 -> 2, of which waited for: 3 -> 2; matrix products, arithmetic and copies ran while one was open for 10% -> 3% of each run, Pallas kernels for 0% -> 0%
where the time goes in v1:
time: 619 us; the launch traced here: 618 us
  waiting for transfers between devices  433 us (70%)
  local copies, waits for them, and re-layouts  88.1 us (14%)
  matrix products  36.1 us (6%)
  blocking collectives  21.6 us (3%)
  other arithmetic  18.5 us (3%)
  between operations  14.2 us (2%)
  starting transfers between devices  6.63 us (1%)
    all_to_all x1, waiting for transfers between devices, per_device(): lax.all_to_all(jnp.stack([integrals] * lax.axis_size('blk')), 'blk', 0, 0)  285 us
    unnamed x2, waiting for transfers between devices  148 us
    select_n x1, local copies, waits for them, and re-layouts, per_device(): jnp.where(int_keep, jnp.concatenate(lax.all_to_all(jnp.stack([integrals]...  30.1 us
    all_to_all x1, blocking collectives, per_device(): lax.all_to_all(amplitudes, 'blk', split_axis=3, concat_axis=1, tiled=True)  21.6 us
    unnamed x14, local copies, waits for them, and re-layouts  21.2 us
    dot_general x1, matrix products, per_device(): jnp.einsum('iakc,kcjb->iajb', sym_amp, sym_piece, precision=lax.Precision...  18.1 us
    dot_general x1, matrix products, per_device(): jnp.einsum('icka,kcjb->iajb', sym_moved, sym_piece, precision=lax.Precisi...  18 us
    reshape x1, local copies, waits for them, and re-layouts, per_device(): jnp.concatenate(lax.all_to_all(jnp.stack([integrals] * lax.axis_size('blk...  13.2 us
  transfers between devices with their start and end apart: 2, of which 2 were waited for; matrix products, arithmetic and copies ran while one was open for 3% of the time, Pallas kernels for 0%

profile of v1, /device:TPU:2, one launch (start us, length us, event | category | flops | bytes accessed | tf_op | source)
XLA Modules:
  0.0 618.1 jit_solution(3457508126714796343)
XLA Ops:
  6.5 4.9 copy.52
  11.4 7.0 %reshape.178 = f32[32,1,5776]{2,1,0:T(1,128)S(1)} reshape(f32[608,4,4,19]{3,2,1,0:T(4,128)} %bitcast.45) | data formatting | bytes 1478656
  18.4 21.6 %all_to_all.23 = f32[32,1,5776]{2,1,0:T(1,128)S(1)} all-to-all(f32[32,1,5776]{2,1,0:T(1,128)S(1)} %reshape.178), channel_id=1, replica_groups=mesh['blk'=32,'int'=16] {'blk'}, dimensions={0} | all-to-all | bytes 1478656 | tf_op jit(solution)/shard_map/all_to_all | solution.py:30
  40.0 9.9 %stack.8 = f32[32,4,608,4,19]{2,3,4,1,0:T(4,128)} broadcast(f32[4,608,4,19]{1,2,3,0:T(4,128)} %param.7), dimensions={1,2,3,4} | broadcast | bytes 24397824 | tf_op jit(solution)/shard_map/stack | solution.py:39
  49.9 0.0 copy-start.2
  49.9 0.0 copy-start.3
  49.9 0.0 copy-start.4
  49.9 0.0 copy-start.1
  49.9 0.0 copy-start
  49.9 6.6 %all-to-all-start = ((f32[32,4,608,4,19]{2,3,4,1,0:T(4,128)}), f32[32,4,608,4,19]{2,3,4,1,0:T(4,128)}, u32[]{:S(2)}, u32[]{:S(2)}) async-start(f32[32,4,608,4,19]{2,3,4,1,0:T(4,128)} %stack.8), calls=%async_computation | async-start | bytes 49807360 | tf_op jit(solution)/shard_map/all_to_all | solution.py:39
  56.5 0.0 all-reduce.3.cloned.1.call-start
  56.5 0.0 copy-done.2
  56.5 0.1 dynamic_slice.6
  56.6 0.0 copy-done.3
  56.6 0.0 copy-done.4
  56.6 0.2 select_reduce_fusion.1
  56.8 0.0 copy-done.1
  56.9 0.1 broadcast_xor_fusion.3
  56.9 0.2 copy.48
  57.1 0.1 dynamic_slice.7
  57.2 0.1 broadcast_xor_fusion.4
  57.3 0.1 broadcast_xor_fusion
  57.3 0.1 broadcast_xor_fusion.1
  57.4 0.0 copy-done
  57.4 0.2 select_bitcast_fusion.1
  57.7 0.5 broadcast.126
  58.2 2.4 reduce
  60.6 8.0 %reshape.179 = f32[608,4,4,19]{3,2,1,0:T(4,128)} reshape(f32[32,5776]{1,0:T(8,128)S(1)} %reduce) | data formatting | bytes 1478656
  68.7 6.2 %copy.75 = f32[4,19,4,32,19]{1,3,2,4,0:T(8,128)} copy(f32[4,19,4,32,19]{1,2,0,4,3:T(4,128)} %bitcast.43) | data formatting | bytes 1478656 | tf_op jit(solution)/shard_map/all_to_all | solution.py:30
  74.9 6.0 all_to_all.20
  80.9 0.3 select_bitcast_fusion
  81.1 285.4 %all-to-all-done = f32[32,4,608,4,19]{2,3,4,1,0:T(4,128)} async-done(((f32[32,4,608,4,19]{2,3,4,1,0:T(4,128)}), f32[32,4,608,4,19]{2,3,4,1,0:T(4,128)}, u32[]{:S(2)}, u32[]{:S(2)}) %all-to-all-start) | async-done | bytes 23658528 | tf_op jit(solution)/shard_map/all_to_all | solution.py:39
  366.5 13.2 %copy.49 = f32[4,608,4,32,19]{1,2,4,3,0:T(4,128)S(1)} copy(f32[4,608,4,32,19]{1,2,4,0,3:T(4,128)} %bitcast.1) | data formatting | bytes 47316992 | tf_op jit(solution)/shard_map/reshape | solution.py:38
  379.8 12.4 %compare_select_fusion = f32[4,608,4,608]{1,2,3,0:T(4,128)} fusion(f32[4,608,4,608]{1,2,3,0:T(4,128)S(1)} %bitcast.42, s32[4,608]{0,1:T(8,128)S(1)} %copy.48, s32[4,608]{1,0:T(4,128)S(1)} %get-tuple-element.7), kind=kLoop, calls=%fused_computation.4 | loop fusion | flops 11829248 | bytes 47336448 | tf_op jit(solution)/shard_map/jit(_where)/select_n | solution.py:36
  392.2 30.1 %copy.51 = f32[4,608,4,608]{3,1,0,2:T(8,128)} copy(f32[4,608,4,608]{1,2,3,0:T(4,128)} %compare_select_fusion) | data formatting | bytes 47316992 | tf_op jit(solution)/shard_map/jit(_where)/select_n | solution.py:36
  422.3 18.0 %fusion.7 = f32[1,4,19,4,608]{4,2,3,1,0:T(8,128)S(1)} fusion(f32[4,608,4,608]{3,1,0,2:T(8,128)} %copy.51, f32[4,608,4,19,1]{1,2,3,0,4:T(4,128)S(1)} %select_bitcast_fusion), kind=kOutput, calls=%fused_computation.8 | convolution fusion | flops 5394137088 | bytes 25137152 | tf_op jit(solution)/shard_map/icka,kcjb->iajb/dot_general | solution.py:44
  440.3 18.1 %fusion.4 = f32[1,4,19,4,608]{4,2,3,1,0:T(8,128)S(1)} fusion(f32[4,608,4,608]{3,1,0,2:T(8,128)} %copy.51, f32[4,19,4,608,1]{3,2,1,0,4:T(4,128)S(1)} %select_bitcast_fusion.1), kind=kOutput, calls=%fused_computation.7 | convolution fusion | flops 5394137088 | bytes 25137152 | tf_op jit(solution)/shard_map/iakc,kcjb->iajb/dot_general | solution.py:43
  458.4 1.4 pad_maximum_fusion
  459.8 0.0 all-reduce.3.cloned.1.call-update
  459.8 1.3 dynamic-slice
  461.8 147.5 %all-reduce.3.cloned.1.call-done = f32[2,4,19,4,608]{4,2,3,1,0:T(8,128)} async-done(((f32[2,4,19,4,608]{4,2,3,1,0:T(8,128)}), f32[2,4,19,4,608]{4,2,3,1,0:T(8,128)}) %all-reduce.3.cloned.1.call-update) | async-done | bytes 1478672
  609.3 1.3 fusion.12
  610.5 0.7 copy.57
Async XLA Ops:
  49.9 6.7 %copy-start.2 = (s32[64]{0:T(128)S(1)}, s32[64]{0:T(128)}, u32[]{:S(2)}) copy-start(s32[64]{0:T(128)} %param.8) | copy-start | bytes 772
  49.9 6.8 %copy-start.3 = (s32[4]{0:T(128)S(1)}, s32[4]{0:T(128)}, u32[]{:S(2)}) copy-start(s32[4]{0:T(128)} %param.10) | copy-start | bytes 52
  49.9 6.8 %copy-start.4 = (s32[4]{0:T(128)S(1)}, s32[4]{0:T(128)}, u32[]{:S(2)}) copy-start(s32[4]{0:T(128)} %param.11) | copy-start | bytes 52
  49.9 7.0 %copy-start.1 = (s32[608]{0:T(1024)S(1)}, s32[608]{0:T(1024)}, u32[]{:S(2)}) copy-start(s32[608]{0:T(1024)} %param.9) | copy-start | bytes 7300
  49.9 7.5 %copy-start = (f32[4,19,4,608]{3,2,1,0:T(4,128)S(1)}, f32[4,19,4,608]{3,2,1,0:T(4,128)}, u32[]{:S(2)}) copy-start(f32[4,19,4,608]{3,2,1,0:T(4,128)} %param.6) | copy-start | bytes 2217988
  49.9 316.7 %all-to-all-start = ((f32[32,4,608,4,19]{2,3,4,1,0:T(4,128)}), f32[32,4,608,4,19]{2,3,4,1,0:T(4,128)}, u32[]{:S(2)}, u32[]{:S(2)}) async-start(f32[32,4,608,4,19]{2,3,4,1,0:T(4,128)} %stack.8), calls=%async_computation | async-start | bytes 49807360 | tf_op jit(solution)/shard_map/all_to_all | solution.py:39
  56.5 552.8 %all-reduce.3.cloned.1.call-start = ((), (), s32[]{:S(2)}) async-start(), calls=%async_computation.2 | async-start | bytes 3932160
Sparse Core Ops, SparseCore 0:
  460.0 149.2 all-reduce.2
